TPU v7x, 256 devices: a whole 4x4x8 slice. The times are simulated.
256 devices in a mesh: row: 16 (over y, x), col: 8 (over z), chan: 2 (over core).
Axes of the slice: x: 4, y: 4, z: 8, core: 2. Of those that a mesh axis runs over, the one named last changes fastest.
Arguments:
- samples: bfloat16 [8192, 2, 8192], P(('chan', 'col'), None, 'row'), parts along dimension 0, may hold values from -6 to 6
- sky_model: bfloat16 [8192, 2, 4096], P(('chan', 'row'), None, 'col'), parts along dimension 0, may hold values from -128 to 128, as said below
- initial_gains: float32 [2, 8192], P(None, ('chan', 'row', 'col')), parts along dimension 1, may hold values from -3 to 3, as said below
Outputs:
- calibrated: float32 [2, 8192], P(None, ('chan', 'row', 'col')), parts along dimension 1
There are 2 independent parts, one for each index of `chan`. A program takes and returns all parts, laid end to end along the dimension named above; each array names one. Nothing has to cross between parts.
Inputs may be any that keep to these rules, and one draw needn't show every extreme that they name: sky_model is Hermitian: sky_model[q,0,p] = sky_model[p,0,q] and sky_model[q,1,p] = -sky_model[p,1,q]. `initial_gains`: every initial gain has magnitude between 0.3 and 3.
All inputs are finite; a program needn't handle non-finite values.
Results may differ from a plain program's by a relative error of at most 0.0003.
Values may be sent and summed in bfloat16 or wider, within the bound.
No kernel may reach another device: no remote copies, remote signals or barrier semaphores. Data moves between devices by JAX's collectives and lax.ppermute only.
A program may use at most 192 MiB of HBM per device.

v0:
```python
import jax
import jax.numpy as jnp
from jax import lax
from jax.sharding import PartitionSpec as P

ITERS = 3


def body(samples, sky_model, initial_gains):
    row_count = lax.axis_size("row")
    column_count = lax.axis_size("col")
    row_index = lax.axis_index("row")
    column_index = lax.axis_index("col")
    block_column = samples.shape[0]
    block_row = sky_model.shape[0]
    share_size = initial_gains.shape[1]
    contract_last = (((1,), (1,)), ((), ()))
    upper_limit = lax.Precision.HIGHEST
    own_start = (row_index * column_count + column_index) * share_size
    flattened = samples.reshape(block_column, -1)
    rotated = jnp.concatenate([-samples[:, 1, :], samples[:, 0, :]], axis=1)
    right_side = jnp.concatenate([flattened, rotated], axis=0)
    all_antennas = lax.all_gather(flattened, "col", axis=0, tiled=True)
    vis_tile = lax.psum_scatter(
        lax.dot_general(
            all_antennas, right_side, contract_last, preferred_element_type=jnp.float32
        ),
        "row",
        scatter_dimension=0,
        tiled=True,
    )
    vis_real = vis_tile[:, :block_column]
    vis_imag = vis_tile[:, block_column:]
    model_real = sky_model[:, 0, :].astype(jnp.float32)
    model_imag = sky_model[:, 1, :].astype(jnp.float32)
    global_rows = row_index * block_row + lax.broadcasted_iota(
        jnp.int32, (block_row, block_column), 0
    )
    global_columns = column_index * block_column + lax.broadcasted_iota(
        jnp.int32, (block_row, block_column), 1
    )
    cross_mask = (global_rows != global_columns).astype(jnp.float32)
    weight_real = (vis_real * model_real + vis_imag * model_imag) * cross_mask
    weight_imag = (vis_real * model_imag - vis_imag * model_real) * cross_mask
    model_power = (model_real * model_real + model_imag * model_imag) * cross_mask
    stacked = jnp.concatenate([weight_real, weight_imag], axis=0)
    row_gains = lax.all_gather(initial_gains, "col", axis=1, tiled=True)
    everything = row_gains
    for iteration in range(ITERS):
        gain_real = row_gains[0]
        gain_imag = row_gains[1]
        left_rows = jnp.stack(
            [jnp.concatenate([gain_real, -gain_imag]), jnp.concatenate([gain_imag, gain_real])]
        )
        totals = jnp.dot(left_rows, stacked, precision=upper_limit)
        energy = jnp.dot(
            gain_real * gain_real + gain_imag * gain_imag, model_power, precision=upper_limit
        )
        totals, energy = (totals, energy)
        totals, energy = (
            lax.psum_scatter(totals, "row", scatter_dimension=1, tiled=True),
            lax.psum_scatter(energy, "row", scatter_dimension=0, tiled=True),
        )
        updated = totals / energy[None, :]
        if iteration == 1:
            previous = lax.dynamic_slice_in_dim(
                everything, (column_index * row_count + row_index) * share_size, share_size, 1
            )
            updated = 0.5 * (updated + previous)
        gain_block = lax.all_gather(updated, "row", axis=1, tiled=True)
        everything = lax.all_gather(gain_block, "col", axis=1, tiled=True)
        row_gains = lax.dynamic_slice_in_dim(everything, row_index * block_row, block_row, 1)
    return lax.dynamic_slice_in_dim(everything, own_start, share_size, 1)


def solution(mesh):
    return jax.shard_map(
        body,
        mesh=mesh,
        in_specs=(
            P(("chan", "col"), None, "row"),
            P(("chan", "row"), None, "col"),
            P(None, ("chan", "row", "col")),
        ),
        out_specs=P(None, ("chan", "row", "col")),
        check_vma=False,
    )
```

profile of v0, /device:TPU:64, one launch (start us, length us, event | category | flops | bytes accessed | tf_op | source)
XLA Modules:
  0.0 626.5 jit_solution(196961169140078920)
XLA Ops:
  6.5 2.5 copy.41
  9.1 0.0 reduce-scatter.11.cloned.1.call-start
  9.2 1.5 fusion.48
  10.7 0.1 copy_bitcast_fusion
  10.8 93.0 %all-gather.6.cloned.1.call-done = bf16[4096,1024]{1,0:T(8,128)(2,1)} async-done(((bf16[512,1024]{1,0:T(8,128)(2,1)}), bf16[4096,1024]{1,0:T(8,128)(2,1)}) %all-gather.6.cloned.1.call-update) | async-done | bytes 8388624 | tf_op jit(solution)/shard_map/all_gather | solution.py:23
  103.8 14.5 %convolution_bitcast_fusion = f32[4096,1024]{0,1:T(8,128)} fusion(bf16[4096,1024]{1,0:T(8,128)(2,1)} %all-gather.6.cloned.1.call-done, bf16[512,512]{1,0:T(8,128)(2,1)S(1)} %get-tuple-element.23, bf16[512,512]{1,0:T(8,128)(2,1)S(1)} %get-tuple-element.24, bf16[512,1024]{1,0:T(8,128)(2,1)S(1)} %bitcast.104), kind=kOutput, calls=%fused_computation | convolution fusion | flops 8596226048 | bytes 27262976 | tf_op jit(solution)/shard_map/dot_general | solution.py:25
  118.3 0.0 reduce-scatter.13.cloned.1.call-start
  118.4 1.0 copy-done.2
  119.3 0.7 fusion.49
  120.1 0.5 copy.39
  120.6 0.5 copy.40
  121.1 14.9 %all-gather = f32[8,32,2]{1,2,0:T(2,128)S(1)} all-gather(f32[1,32,2]{1,2,0:T(2,128)S(1)} %bitcast.131), channel_id=1, replica_groups=mesh['row'=16,'col'=8,'chan'=2] {'col'}, dimensions={0}, use_global_device_ids=true | all-gather | bytes 2304 | tf_op jit(solution)/shard_map/all_gather | solution.py:47
  135.9 0.1 reshape.72
  136.0 98.7 %reduce-scatter.11.cloned.1.call-done = f32[256,1024]{0,1:T(8,128)} async-done(((f32[4096,1024]{0,1:T(8,128)}), f32[256,1024]{0,1:T(8,128)}) %reduce-scatter.11.cloned.1.call-update) | async-done | bytes 1048592 | tf_op jit(solution)/shard_map/reduce_scatter | solution.py:24
  234.7 1.4 compare_select_fusion.1
  236.1 1.7 convolution_bitcast_fusion.3
  237.9 0.7 fusion.28
  238.5 0.6 dynamic-slice
  239.8 38.1 %all-reduce = f32[512]{0:T(512)S(1)} all-reduce(f32[512]{0:T(512)S(1)} %bitcast.128), channel_id=4, replica_groups=mesh['row'=16,'col'=8,'chan'=2] {'row'}, use_global_device_ids=true, to_apply=%region_2.0.clone | all-reduce | flops 512 | bytes 4096
  277.9 0.1 dynamic-slice.1
  278.0 37.9 %reduce-scatter.13.cloned.1.call-done = f32[32,2]{1,0:T(8,128)} async-done(((f32[512,2]{1,0:T(8,128)}), f32[32,2]{1,0:T(8,128)}) %reduce-scatter.13.cloned.1.call-update) | async-done | bytes 272
  315.8 0.8 copy.32
  316.6 22.7 %all-gather.1 = f32[16,32,2]{1,2,0:T(2,128)S(1)} all-gather(f32[1,32,2]{1,2,0:T(2,128)S(1)} %divide_bitcast_fusion.1), channel_id=1, replica_groups=mesh['row'=16,'col'=8,'chan'=2] {'row'}, dimensions={0}, use_global_device_ids=true | all-gather | bytes 4352 | tf_op jit(solution)/shard_map/all_gather | solution.py:70
  339.4 0.1 reshape.74
  339.4 25.7 %all_gather.27 = f32[2,4096]{1,0:T(2,128)S(1)} all-gather(f32[2,512]{1,0:T(2,128)S(1)} %bitcast.105), channel_id=1, replica_groups=mesh['row'=16,'col'=8,'chan'=2] {'col'}, dimensions={1}, use_global_device_ids=true | all-gather | bytes 36864 | tf_op jit(solution)/shard_map/all_gather | solution.py:71
  365.2 0.1 fusion.51
  365.3 1.7 convolution_bitcast_fusion.2
  367.0 0.0 reduce-scatter.17.cloned.1.call-start
  367.0 0.6 fusion.26
  367.6 38.1 %all-reduce.1 = f32[512]{0:T(512)S(1)} all-reduce(f32[512]{0:T(512)S(1)} %bitcast.130), channel_id=6, replica_groups=mesh['row'=16,'col'=8,'chan'=2] {'row'}, use_global_device_ids=true, to_apply=%region_4.0.clone | all-reduce | flops 512 | bytes 4096
  405.8 0.1 dynamic-slice.3
  405.9 37.0 %reduce-scatter.15.cloned.1.call-done = f32[32,2]{1,0:T(8,128)} async-done(((f32[512,2]{1,0:T(8,128)}), f32[32,2]{1,0:T(8,128)}) %reduce-scatter.15.cloned.1.call-update) | async-done | bytes 272
  442.9 0.8 copy.34
  443.7 0.1 multiply_bitcast_fusion
  443.8 22.7 %all-gather.2 = f32[16,32,2]{1,2,0:T(2,128)S(1)} all-gather(f32[1,32,2]{1,2,0:T(2,128)S(1)} %multiply_bitcast_fusion), channel_id=1, replica_groups=mesh['row'=16,'col'=8,'chan'=2] {'row'}, dimensions={0}, use_global_device_ids=true | all-gather | bytes 4352 | tf_op jit(solution)/shard_map/all_gather | solution.py:70
  466.5 0.1 reshape.76
  466.6 25.7 %all_gather.29 = f32[2,4096]{1,0:T(2,128)S(1)} all-gather(f32[2,512]{1,0:T(2,128)S(1)} %bitcast.106), channel_id=1, replica_groups=mesh['row'=16,'col'=8,'chan'=2] {'col'}, dimensions={1}, use_global_device_ids=true | all-gather | bytes 36864 | tf_op jit(solution)/shard_map/all_gather | solution.py:71
  492.3 0.1 fusion.50
  492.4 1.7 convolution_bitcast_fusion.1
  494.1 0.6 fusion.24
  494.7 38.1 %all-reduce.2 = f32[512]{0:T(512)S(1)} all-reduce(f32[512]{0:T(512)S(1)} %bitcast.129), channel_id=8, replica_groups=mesh['row'=16,'col'=8,'chan'=2] {'row'}, use_global_device_ids=true, to_apply=%region_6.0.clone | all-reduce | flops 512 | bytes 4096
  532.8 0.1 dynamic-slice.5
  532.9 37.1 %reduce-scatter.17.cloned.1.call-done = f32[32,2]{1,0:T(8,128)} async-done(((f32[512,2]{1,0:T(8,128)}), f32[32,2]{1,0:T(8,128)}) %reduce-scatter.17.cloned.1.call-update) | async-done | bytes 272
  570.0 0.8 copy.36
  570.8 22.7 %all-gather.3 = f32[16,32,2]{1,2,0:T(2,128)S(1)} all-gather(f32[1,32,2]{1,2,0:T(2,128)S(1)} %divide_bitcast_fusion), channel_id=1, replica_groups=mesh['row'=16,'col'=8,'chan'=2] {'row'}, dimensions={0}, use_global_device_ids=true | all-gather | bytes 4352 | tf_op jit(solution)/shard_map/all_gather | solution.py:70
  593.5 0.1 reshape.78
  593.6 25.7 %all_gather.31 = f32[2,4096]{1,0:T(2,128)S(1)} all-gather(f32[2,512]{1,0:T(2,128)S(1)} %bitcast.107), channel_id=1, replica_groups=mesh['row'=16,'col'=8,'chan'=2] {'col'}, dimensions={1}, use_global_device_ids=true | all-gather | bytes 36864 | tf_op jit(solution)/shard_map/all_gather | solution.py:71
  619.3 0.6 constant_dynamic-slice_fusion.1
  (31 shorter events, 0.2 us)
Async XLA Ops:
  6.5 2.6 copy-start
  6.5 97.2 %all-gather.6.cloned.1.call-start = ((), (), s32[]{:S(2)}) async-start(), calls=%async_computation.4 | async-start | bytes 9437184 | tf_op jit(solution)/shard_map/all_gather | solution.py:23
  9.1 94.7 %copy-start.1 = (bf16[64,8,2,512]{3,1,2,0:T(8,128)(2,1)S(1)}, bf16[64,8,2,512]{3,1,2,0:T(8,128)(2,1)}, u32[]{:S(2)}) copy-start(bf16[64,8,2,512]{3,1,2,0:T(8,128)(2,1)} %copy.41) | copy-start | bytes 3145732
  9.1 225.6 %reduce-scatter.11.cloned.1.call-start = ((), (), s32[]{:S(2)}) async-start(), calls=%async_computation.5 | async-start | bytes 17825792 | tf_op jit(solution)/shard_map/reduce_scatter | solution.py:24
  118.3 1.0 copy-start.2
  118.3 2.7 copy-start.3
  118.3 197.5 %reduce-scatter.13.cloned.1.call-start = ((), (), s32[]{:S(2)}) async-start(), calls=%async_computation.6 | async-start | bytes 278528
  119.3 119.2 %copy-start.4 = (u32[256]{0:T(256)S(1)}, u32[256]{0:T(256)}, u32[]{:S(2)}) copy-start(u32[256]{0:T(256)} %constant.34) | copy-start | bytes 3076
  237.8 205.1 %reduce-scatter.15.cloned.1.call-start = ((), (), s32[]{:S(2)}) async-start(), calls=%async_computation.7 | async-start | bytes 278528
  367.0 203.0 %reduce-scatter.17.cloned.1.call-start = ((), (), s32[]{:S(2)}) async-start(), calls=%async_computation.8 | async-start | bytes 278528
Sparse Core Ops, SparseCore 0:
  9.2 94.5 all-gather.5
  118.4 116.2 reduce-scatter.10
  238.2 77.6 reduce-scatter.12
  367.1 75.7 reduce-scatter.14
  494.2 75.7 reduce-scatter.16
where the time goes:
time: 627 us; the launch traced here: 626 us
  waiting for transfers between devices  304 us (48%)
  blocking collectives  275 us (44%)
  matrix products  21.5 us (3%)
  between operations  13.9 us (2%)
  local copies, waits for them, and re-layouts  11 us (2%)
    unnamed x3, blocking collectives  114 us
    unnamed x8, waiting for transfers between devices  112 us
    reduce_scatter x1, waiting for transfers between devices, body(): lax.psum_scatter(lax.dot_general(all_antennas, right_side, contract_last,...  98.7 us
    all_gather x1, waiting for transfers between devices, body(): all_antennas = lax.all_gather(flattened, 'col', axis=0, tiled=True)  93 us
    all_gather x3, blocking collectives, body(): everything = lax.all_gather(gain_block, 'col', axis=1, tiled=True)  77.2 us
    all_gather x3, blocking collectives, body(): gain_block = lax.all_gather(updated, 'row', axis=1, tiled=True)  68.1 us
    all_gather x1, blocking collectives, body(): row_gains = lax.all_gather(initial_gains, 'col', axis=1, tiled=True)  14.9 us
    dot_general x1, matrix products, body(): lax.dot_general(all_antennas, right_side, contract_last, preferred_elemen...  14.5 us
  transfers between devices with their start and end apart: 5, of which 5 were waited for; matrix products, arithmetic and copies ran while one was open for 1% of the time, Pallas kernels for 0%

commit v1 on v0

--- a/solution.py
+++ b/solution.py
@@ -67,7 +67,9 @@
                 everything, (column_index * row_count + row_index) * share_size, share_size, 1
             )
             updated = 0.5 * (updated + previous)
-        gain_block = lax.all_gather(updated, "row", axis=1, tiled=True)
+        gain_block = jnp.concatenate(
+            lax.all_to_all(jnp.stack([updated] * lax.axis_size("row")), "row", 0, 0), axis=1
+        )
         everything = lax.all_gather(gain_block, "col", axis=1, tiled=True)
         row_gains = lax.dynamic_slice_in_dim(everything, row_index * block_row, block_row, 1)
     return lax.dynamic_slice_in_dim(everything, own_start, share_size, 1)

time: 627 us -> 596 us (0.951)
  blocking collectives: 275 us -> 217 us
  waiting for transfers between devices: 304 us -> 319 us
  starting transfers between devices: 0.17 us -> 10.1 us
    all_gather x3 -> x0, blocking collectives: 68.1 us -> none  [body(): gain_block = lax.all_gather(updated, 'row', axis=1, tiled=True)]
    all_to_all x0 -> x2, waiting for transfers between devices: none -> 15.1 us  [body(): lax.all_to_all(jnp.stack([updated] * lax.axis_size('row')), 'row', 0, 0)]
    all_to_all x0 -> x1, blocking collectives: none -> 12.3 us  [body(): lax.all_to_all(jnp.stack([updated] * lax.axis_size('row')), 'row', 0, 0)]
    all_to_all x0 -> x2, starting transfers between devices: none -> 9.88 us  [body(): lax.all_to_all(jnp.stack([updated] * lax.axis_size('row')), 'row', 0, 0)]
  transfers between devices with their start and end apart: 5 -> 7, of which waited for: 5 -> 7; matrix products, arithmetic and copies ran while one was open for 1% -> 1% of each run, Pallas kernels for 0% -> 0%
where the time goes in v1:
time: 596 us; the launch traced here: 595 us
  waiting for transfers between devices  319 us (54%)
  blocking collectives  217 us (36%)
  matrix products  21.4 us (4%)
  between operations  13.9 us (2%)
  local copies, waits for them, and re-layouts  12.3 us (2%)
  starting transfers between devices  10.1 us (2%)
    unnamed x3, blocking collectives  113 us
    unnamed x8, waiting for transfers between devices  112 us
    reduce_scatter x1, waiting for transfers between devices, body(): lax.psum_scatter(lax.dot_general(all_antennas, right_side, contract_last,...  98.6 us
    all_gather x1, waiting for transfers between devices, body(): all_antennas = lax.all_gather(flattened, 'col', axis=0, tiled=True)  93 us
    all_gather x3, blocking collectives, body(): everything = lax.all_gather(gain_block, 'col', axis=1, tiled=True)  77.2 us
    all_to_all x2, waiting for transfers between devices, body(): lax.all_to_all(jnp.stack([updated] * lax.axis_size('row')), 'row', 0, 0)  15.1 us
    all_gather x1, blocking collectives, body(): row_gains = lax.all_gather(initial_gains, 'col', axis=1, tiled=True)  14.9 us
    dot_general x1, matrix products, body(): lax.dot_general(all_antennas, right_side, contract_last, preferred_elemen...  14.5 us
  transfers between devices with their start and end apart: 7, of which 7 were waited for; matrix products, arithmetic and copies ran while one was open for 1% of the time, Pallas kernels for 0%

profile of v1, /device:TPU:64, one launch (start us, length us, event | category | flops | bytes accessed | tf_op | source)
XLA Modules:
  0.0 595.3 jit_solution(14023769056051089342)
XLA Ops:
  6.5 2.5 copy.36
  9.2 1.5 fusion.49
  10.7 0.1 copy_bitcast_fusion
  10.8 93.0 %all-gather.3.cloned.1.call-done = bf16[4096,1024]{1,0:T(8,128)(2,1)} async-done(((bf16[512,1024]{1,0:T(8,128)(2,1)}), bf16[4096,1024]{1,0:T(8,128)(2,1)}) %all-gather.3.cloned.1.call-update) | async-done | bytes 8388624 | tf_op jit(solution)/shard_map/all_gather | solution.py:23
  103.8 14.5 %convolution_bitcast_fusion = f32[4096,1024]{0,1:T(8,128)} fusion(bf16[4096,1024]{1,0:T(8,128)(2,1)} %all-gather.3.cloned.1.call-done, bf16[512,512]{1,0:T(8,128)(2,1)S(1)} %get-tuple-element.23, bf16[512,512]{1,0:T(8,128)(2,1)S(1)} %get-tuple-element.24, bf16[512,1024]{1,0:T(8,128)(2,1)S(1)} %bitcast.86), kind=kOutput, calls=%fused_computation | convolution fusion | flops 8596226048 | bytes 27262976 | tf_op jit(solution)/shard_map/dot_general | solution.py:25
  118.3 1.0 copy-done.2
  119.3 0.7 fusion.50
  120.0 0.5 copy.34
  120.5 0.5 copy.35
  121.0 14.9 %all-gather = f32[8,32,2]{1,2,0:T(2,128)S(1)} all-gather(f32[1,32,2]{1,2,0:T(2,128)S(1)} %bitcast.113), channel_id=1, replica_groups=mesh['row'=16,'col'=8,'chan'=2] {'col'}, dimensions={0}, use_global_device_ids=true | all-gather | bytes 2304 | tf_op jit(solution)/shard_map/all_gather | solution.py:47
  135.9 0.1 reshape.102
  136.0 98.6 %reduce-scatter.11.cloned.1.call-done = f32[256,1024]{0,1:T(8,128)} async-done(((f32[4096,1024]{0,1:T(8,128)}), f32[256,1024]{0,1:T(8,128)}) %reduce-scatter.11.cloned.1.call-update) | async-done | bytes 1048592 | tf_op jit(solution)/shard_map/reduce_scatter | solution.py:24
  234.6 1.4 compare_select_fusion.1
  236.0 1.7 convolution_bitcast_fusion.3
  237.7 0.7 fusion.28
  238.4 0.6 dynamic-slice
  239.6 38.1 %all-reduce = f32[512]{0:T(512)S(1)} all-reduce(f32[512]{0:T(512)S(1)} %bitcast.110), channel_id=4, replica_groups=mesh['row'=16,'col'=8,'chan'=2] {'row'}, use_global_device_ids=true, to_apply=%region_2.0.clone | all-reduce | flops 512 | bytes 4096
  277.8 0.1 dynamic-slice.1
  277.9 38.0 %reduce-scatter.13.cloned.1.call-done = f32[32,2]{1,0:T(8,128)} async-done(((f32[512,2]{1,0:T(8,128)}), f32[32,2]{1,0:T(8,128)}) %reduce-scatter.13.cloned.1.call-update) | async-done | bytes 272
  315.8 0.8 copy.27
  316.6 0.6 stack.27
  317.2 4.9 all-to-all-start
  322.2 7.5 %all-to-all-done = f32[16,2,32]{2,1,0:T(2,128)S(1)} async-done(((f32[16,2,32]{2,1,0:T(2,128)}), f32[16,2,32]{2,1,0:T(2,128)S(1)}, u32[]{:S(2)}, u32[]{:S(2)}) %all-to-all-start) | async-done | bytes 4128 | tf_op jit(solution)/shard_map/all_to_all | solution.py:71
  329.8 0.1 reshape.94
  329.9 25.7 %all_gather.17 = f32[2,4096]{1,0:T(2,128)S(1)} all-gather(f32[2,512]{1,0:T(2,128)S(1)} %reshape.94), channel_id=1, replica_groups=mesh['row'=16,'col'=8,'chan'=2] {'col'}, dimensions={1}, use_global_device_ids=true | all-gather | bytes 36864 | tf_op jit(solution)/shard_map/all_gather | solution.py:73
  355.6 0.1 fusion.52
  355.7 1.7 convolution_bitcast_fusion.2
  357.4 0.6 fusion.26
  358.1 37.3 %all-reduce.1 = f32[512]{0:T(512)S(1)} all-reduce(f32[512]{0:T(512)S(1)} %bitcast.112), channel_id=6, replica_groups=mesh['row'=16,'col'=8,'chan'=2] {'row'}, use_global_device_ids=true, to_apply=%region_4.0.clone | all-reduce | flops 512 | bytes 4096
  395.3 0.1 dynamic-slice.3
  395.4 37.1 %reduce-scatter.15.cloned.1.call-done = f32[32,2]{1,0:T(8,128)} async-done(((f32[512,2]{1,0:T(8,128)}), f32[32,2]{1,0:T(8,128)}) %reduce-scatter.15.cloned.1.call-update) | async-done | bytes 272
  432.5 0.8 copy.29
  433.3 0.1 fusion.39
  433.3 12.3 %all_to_all.15 = f32[16,2,32]{2,1,0:T(2,128)S(1)} all-to-all(f32[16,2,32]{2,1,0:T(2,128)S(1)} %stack.31), channel_id=1, replica_groups=mesh['row'=16,'col'=8,'chan'=2] {'row'}, dimensions={0} | all-to-all | bytes 8192 | tf_op jit(solution)/shard_map/all_to_all | solution.py:71
  445.7 0.1 reshape.96
  445.8 25.7 %all_gather.18 = f32[2,4096]{1,0:T(2,128)S(1)} all-gather(f32[2,512]{1,0:T(2,128)S(1)} %reshape.96), channel_id=1, replica_groups=mesh['row'=16,'col'=8,'chan'=2] {'col'}, dimensions={1}, use_global_device_ids=true | all-gather | bytes 36864 | tf_op jit(solution)/shard_map/all_gather | solution.py:73
  471.6 1.7 convolution_bitcast_fusion.1
  473.3 0.6 fusion.24
  473.9 37.3 %all-reduce.2 = f32[512]{0:T(512)S(1)} all-reduce(f32[512]{0:T(512)S(1)} %bitcast.111), channel_id=8, replica_groups=mesh['row'=16,'col'=8,'chan'=2] {'row'}, use_global_device_ids=true, to_apply=%region_6.0.clone | all-reduce | flops 512 | bytes 4096
  511.2 0.1 dynamic-slice.5
  511.2 37.1 %reduce-scatter.17.cloned.1.call-done = f32[32,2]{1,0:T(8,128)} async-done(((f32[512,2]{1,0:T(8,128)}), f32[32,2]{1,0:T(8,128)}) %reduce-scatter.17.cloned.1.call-update) | async-done | bytes 272
  548.4 0.8 copy.31
  549.2 0.6 stack.35
  549.8 4.9 all-to-all-start.2
  554.7 7.6 %all-to-all-done.2 = f32[16,2,32]{2,1,0:T(2,128)S(1)} async-done(((f32[16,2,32]{2,1,0:T(2,128)}), f32[16,2,32]{2,1,0:T(2,128)S(1)}, u32[]{:S(2)}, u32[]{:S(2)}) %all-to-all-start.2) | async-done | bytes 4128 | tf_op jit(solution)/shard_map/all_to_all | solution.py:71
  562.3 0.1 reshape.98
  562.4 25.7 %all_gather.19 = f32[2,4096]{1,0:T(2,128)S(1)} all-gather(f32[2,512]{1,0:T(2,128)S(1)} %reshape.98), channel_id=1, replica_groups=mesh['row'=16,'col'=8,'chan'=2] {'col'}, dimensions={1}, use_global_device_ids=true | all-gather | bytes 36864 | tf_op jit(solution)/shard_map/all_gather | solution.py:73
  588.1 0.6 constant_dynamic-slice_fusion.1
  (36 shorter events, 0.4 us)
Async XLA Ops:
  6.5 2.6 copy-start
  6.5 97.2 %all-gather.3.cloned.1.call-start = ((), (), s32[]{:S(2)}) async-start(), calls=%async_computation.7 | async-start | bytes 9437184 | tf_op jit(solution)/shard_map/all_gather | solution.py:23
  9.1 94.7 %copy-start.1 = (bf16[64,8,2,512]{3,1,2,0:T(8,128)(2,1)S(1)}, bf16[64,8,2,512]{3,1,2,0:T(8,128)(2,1)}, u32[]{:S(2)}) copy-start(bf16[64,8,2,512]{3,1,2,0:T(8,128)(2,1)} %copy.36) | copy-start | bytes 3145732
  9.1 225.5 %reduce-scatter.11.cloned.1.call-start = ((), (), s32[]{:S(2)}) async-start(), calls=%async_computation.8 | async-start | bytes 17825792 | tf_op jit(solution)/shard_map/reduce_scatter | solution.py:24
  118.2 1.0 copy-start.2
  118.3 2.7 copy-start.3
  118.3 197.5 %reduce-scatter.13.cloned.1.call-start = ((), (), s32[]{:S(2)}) async-start(), calls=%async_computation.9 | async-start | bytes 278528
  119.3 119.1 %copy-start.4 = (u32[256]{0:T(256)S(1)}, u32[256]{0:T(256)}, u32[]{:S(2)}) copy-start(u32[256]{0:T(256)} %constant.34) | copy-start | bytes 3076
  317.2 12.5 %all-to-all-start = ((f32[16,2,32]{2,1,0:T(2,128)}), f32[16,2,32]{2,1,0:T(2,128)S(1)}, u32[]{:S(2)}, u32[]{:S(2)}) async-start(f32[16,2,32]{2,1,0:T(2,128)} %stack.27), calls=%async_computation.1 | async-start | bytes 32768 | tf_op jit(solution)/shard_map/all_to_all | solution.py:71
  322.2 110.3 %reduce-scatter.15.cloned.1.call-start = ((), (), s32[]{:S(2)}) async-start(), calls=%async_computation.10 | async-start | bytes 278528
  357.4 191.0 %reduce-scatter.17.cloned.1.call-start = ((), (), s32[]{:S(2)}) async-start(), calls=%async_computation.11 | async-start | bytes 278528
  549.8 12.5 %all-to-all-start.2 = ((f32[16,2,32]{2,1,0:T(2,128)}), f32[16,2,32]{2,1,0:T(2,128)S(1)}, u32[]{:S(2)}, u32[]{:S(2)}) async-start(f32[16,2,32]{2,1,0:T(2,128)} %stack.35), calls=%async_computation.3 | async-start | bytes 32768 | tf_op jit(solution)/shard_map/all_to_all | solution.py:71
Sparse Core Ops, SparseCore 0:
  9.2 94.5 all-gather.2
  118.4 116.1 reduce-scatter.10
  238.1 77.6 reduce-scatter.12
  357.5 74.9 reduce-scatter.14
  473.4 74.9 reduce-scatter.16
